TPU v7x, 256 devices: a whole 4x4x8 slice. The times are simulated.
256 devices in a mesh: dp: 32 (over x, z), mp: 8 (over y, core).
Axes of the slice: x: 4, y: 4, z: 8, core: 2. Of those that a mesh axis runs over, the one named last changes fastest.
Arguments:
- residual_in: bfloat16 [8192, 5120], P('dp', 'mp'), may hold values from -6 to 6
- queries_in: bfloat16 [8192, 5120], P('dp', 'mp'), may hold values from -360 to 360
- key_values: bfloat16 [2, 8192, 1024], P(None, 'dp', 'mp'), may hold values from -6 to 6
- request_ids: int32 [8192], P('dp'), may hold values from 0 to 8191, as said below
- deal_order: int32 [32], replicated, may hold values from 0 to 31, each once
- page_table: int32 [512], P('dp'), may hold values from 0 to 511, as said below
- out_proj: bfloat16 [5120, 5120], P('dp', 'mp'), may hold values from -0.078125 to 0.078125
- norm_gain: bfloat16 [5120], P('mp'), may hold values from 0.099609375 to 1.8984375
- gate_up: bfloat16 [5120, 2, 16384], P('mp', None, 'dp'), may hold values from -0.078125 to 0.078125
Outputs:
- mlp_hidden: bfloat16 [8192, 16384], P('mp', 'dp')
- kv_cache: bfloat16 [512, 2, 16, 1024], P('dp', None, None, 'mp')
- residual_out: bfloat16 [8192, 5120], P('dp', 'mp')
Inputs may be any that keep to these rules, and one draw needn't show every extreme that they name: `request_ids`: each request lies whole inside one aligned block of 256 packed tokens, which holds one to three requests of 32 tokens or more; its id is the index of its first token. `page_table`: each aligned block of 16 entries is a permutation of that block's own page numbers.
All inputs are finite; a program needn't handle non-finite values.
Results may differ from a plain program's by a relative error of at most 0.02.
Values may be sent and summed in bfloat16 or wider, within the bound.
No kernel may reach another device: no remote copies, remote signals or barrier semaphores. Data moves between devices by JAX's collectives and lax.ppermute only.
A program may use at most 128 MiB of HBM per device.

v0:
```python
import jax
import jax.numpy as jnp
from jax import lax
from jax.sharding import PartitionSpec as P

D = 5120
HD = 128
epsilon = 1e-06


def attend(queries_in, key_values, request_ids):
    tok_rows = queries_in.shape[0]
    q_heads = queries_in.shape[1] // HD
    kv_heads = key_values.shape[2] // HD
    group = q_heads // kv_heads
    queries = queries_in.reshape(tok_rows, kv_heads, group, HD)
    keys = key_values[0].reshape(tok_rows, kv_heads, HD)
    values = key_values[1].reshape(tok_rows, kv_heads, HD)
    scores = jnp.einsum(
        "qhgd,khd->hgqk", queries, keys, preferred_element_type=jnp.float32
    ) * HD ** (-0.5)
    places = jnp.arange(tok_rows, dtype=jnp.int32)
    allowed = (request_ids[:, None] == request_ids[None, :]) & (places[None, :] <= places[:, None])
    scores = jnp.where(allowed, scores, -1e30)
    row_max = jnp.max(scores, axis=-1, keepdims=True)
    lifted = jnp.exp(scores - row_max)
    weights = (lifted / jnp.sum(lifted, axis=-1, keepdims=True)).astype(jnp.bfloat16)
    mixed = jnp.einsum("hgqk,khd->qhgd", weights, values, preferred_element_type=jnp.float32)
    return mixed.astype(jnp.bfloat16).reshape(tok_rows, q_heads * HD)


def shards(
    residual_in,
    queries_in,
    key_values,
    request_ids,
    deal_order,
    page_table,
    out_proj,
    norm_gain,
    gate_up,
):
    tok_rows = residual_in.shape[0]
    local_width = residual_in.shape[1]
    pages_here = page_table.shape[0]
    page_rows = tok_rows // pages_here
    channels = key_values.shape[2]
    pages = key_values.reshape(2, pages_here, page_rows, channels).transpose(1, 0, 2, 3)
    kv_cache = jnp.zeros_like(pages).at[page_table % pages_here].set(pages)
    attended = attend(queries_in, key_values, request_ids)
    all_heads = lax.all_gather(attended, "mp", axis=1, tiled=True)
    projected = jnp.dot(
        all_heads,
        lax.all_gather(out_proj, "dp", axis=0, tiled=True),
        preferred_element_type=jnp.float32,
    )
    resid = residual_in.astype(jnp.float32) + projected
    square_sums = lax.psum(jnp.sum(resid * resid, axis=1), "mp")
    mean_square = square_sums / D
    normed = (
        resid * lax.rsqrt(mean_square + epsilon)[:, None] * norm_gain.astype(jnp.float32)
    ).astype(jnp.bfloat16)
    every_row = lax.all_gather(normed, "dp", axis=0, tiled=True)
    dp_count = lax.axis_size("dp")
    packed_blocks = every_row.reshape(dp_count, tok_rows, local_width)
    hidden_here = gate_up.shape[2]
    flat_weights = gate_up.reshape(local_width, 2 * hidden_here)
    own_rows = every_row.shape[0] // lax.axis_size("mp")
    picked = jnp.take(packed_blocks, deal_order, axis=0).reshape(
        own_rows * lax.axis_size("mp"), local_width
    )
    partial_sum = jnp.dot(picked, flat_weights, preferred_element_type=jnp.float32).astype(
        jnp.bfloat16
    )
    partial_sum = lax.optimization_barrier(partial_sum)
    summed = lax.psum_scatter(
        partial_sum.astype(jnp.float32).astype(jnp.bfloat16), "mp", scatter_dimension=0, tiled=True
    ).astype(jnp.float32)
    mlp_hidden = (jax.nn.silu(summed[:, :hidden_here]) * summed[:, hidden_here:]).astype(
        jnp.bfloat16
    )
    return (mlp_hidden, kv_cache, resid.astype(jnp.bfloat16))


def solution(mesh):
    in_specs = (
        P("dp", "mp"),
        P("dp", "mp"),
        P(None, "dp", "mp"),
        P("dp"),
        P(),
        P("dp"),
        P("dp", "mp"),
        P("mp"),
        P("mp", None, "dp"),
    )
    out_specs = (P("mp", "dp"), P("dp", None, None, "mp"), P("dp", "mp"))
    return jax.shard_map(shards, mesh=mesh, in_specs=in_specs, out_specs=out_specs, check_vma=False)
```

profile of v0, /device:TPU:1, one launch (start us, length us, event | category | flops | bytes accessed | tf_op | source)
XLA Modules:
  0.0 402.9 jit_solution(12429837756996770780)
XLA Ops:
  7.2 0.0 copy-start.3
  7.2 0.0 all-gather.4.cloned.1.call-start
  7.2 1.2 copy.16
  8.4 0.9 fusion.5
  9.3 1.2 fusion.12
  10.5 0.2 fusion.3
  10.7 0.0 copy-start.4
  10.7 0.0 copy-start.2
  10.7 1.1 convolution_convert_fusion.1
  11.8 0.0 all-gather.4.cloned.1.call-update
  11.8 0.0 all-gather.6.cloned.1.call-start
  11.9 0.7 all-gather.6.cloned.1.call-update
  12.6 0.0 all-gather.8.cloned.1.call-start
  12.6 32.1 %all-gather.4.cloned.1.call-done = bf16[256,5120]{0,1:T(8,128)(2,1)} async-done(((bf16[256,640]{0,1:T(8,128)(2,1)}), bf16[256,5120]{0,1:T(8,128)(2,1)}) %all-gather.4.cloned.1.call-update) | async-done | bytes 2621456 | tf_op jit(solution)/shard_map/all_gather | solution.py:51
  44.7 91.6 %all-gather.6.cloned.1.call-done = bf16[5120,640]{1,0:T(8,128)(2,1)} async-done(((bf16[160,640]{1,0:T(8,128)(2,1)}), bf16[5120,640]{1,0:T(8,128)(2,1)}) %all-gather.6.cloned.1.call-update) | async-done | bytes 6553616 | tf_op jit(solution)/shard_map/all_gather | solution.py:54
  136.3 6.0 %multiply_reduce_fusion = (f32[256]{0:T(256)S(1)}, f32[256,640]{1,0:T(8,128)S(1)}) fusion(bf16[256,5120]{0,1:T(8,128)(2,1)} %all-gather.4.cloned.1.call-done, bf16[5120,640]{1,0:T(8,128)(2,1)} %all-gather.6.cloned.1.call-done, bf16[256,640]{1,0:T(8,128)(2,1)S(1)} %copy-done.2), kind=kOutput, calls=%fused_computation.16 | convolution fusion | flops 1678376704 | bytes 10159104 | tf_op jit(solution)/shard_map/dot_general | solution.py:52
  142.3 13.1 %psum.7 = f32[256]{0:T(256)S(1)} all-reduce(f32[256]{0:T(256)S(1)} %get-tuple-element.7), channel_id=1, replica_groups=mesh['dp'=32,'mp'=8] {'mp'}, use_global_device_ids=true, to_apply=%region_3.4 | all-reduce | flops 256 | bytes 2048 | tf_op jit(solution)/shard_map/psum | solution.py:58
  155.4 1.0 fusion.11
  156.4 0.0 all-gather.8.cloned.1.call-update
  156.4 0.0 reduce-scatter.2.cloned.1.call-start
  156.4 0.3 copy.24
  156.8 103.8 %all-gather.8.cloned.1.call-done = bf16[8192,640]{1,0:T(8,128)(2,1)} async-done(((bf16[256,640]{1,0:T(8,128)(2,1)}), bf16[8192,640]{1,0:T(8,128)(2,1)}) %all-gather.8.cloned.1.call-update) | async-done | bytes 10485776 | tf_op jit(solution)/shard_map/all_gather | solution.py:63
  260.6 10.2 %gather_fusion = bf16[32,256,640]{2,1,0:T(8,128)(2,1)} fusion(bf16[32,256,640]{2,1,0:T(8,128)(2,1)} %bitcast.41, s32[1024]{0:T(1024)S(1)} %pad_clamp_fusion), kind=kCustom, calls=%fused_computation | custom fusion | bytes 20971648 | tf_op jit(solution)/shard_map/jit(_take)/gather | solution.py:69
  270.8 10.2 %broadcast_select_fusion = bf16[32,256,640]{2,1,0:T(8,128)(2,1)} fusion(bf16[32,256,640]{2,1,0:T(8,128)(2,1)} %gather_fusion, pred[32]{0:T(512)(128)(4,1)S(1)} %compare_and_fusion), kind=kLoop, calls=%fused_computation.3 | loop fusion | flops 5242880 | bytes 20971552 | tf_op jit(solution)/shard_map/jit(_take)/select_n | solution.py:69
  281.0 19.9 %convolution_convert_fusion = bf16[8192,1024]{1,0:T(8,128)(2,1)} fusion(bf16[8192,640]{1,0:T(8,128)(2,1)} %bitcast.42, bf16[640,1024]{1,0:T(8,128)(2,1)S(1)} %bitcast.45), kind=kOutput, calls=%fused_computation.2 | convolution fusion | flops 10745806848 | bytes 28573696 | tf_op jit(solution)/shard_map/dot_general | solution.py:72
  300.9 0.0 reduce-scatter.2.cloned.1.call-update
  300.9 0.6 copy-done.6
  301.6 1.0 scatter_fusion
  302.6 0.0 copy-start.1
  302.6 90.1 %reduce-scatter.2.cloned.1.call-done = bf16[1024,1024]{1,0:T(8,128)(2,1)} async-done(((bf16[8192,1024]{1,0:T(8,128)(2,1)}), bf16[1024,1024]{1,0:T(8,128)(2,1)}) %reduce-scatter.2.cloned.1.call-update) | async-done | bytes 2097168 | tf_op jit(solution)/shard_map/reduce_scatter | solution.py:76
  392.7 2.0 convert_element_type.47
  394.7 1.7 fusion
  (17 shorter events, 0.1 us)
Async XLA Ops:
  7.2 3.5 copy-start.3
  7.2 37.5 %all-gather.4.cloned.1.call-start = ((), (), s32[]{:S(2)}) async-start(), calls=%async_computation.1 | async-start | bytes 2949120 | tf_op jit(solution)/shard_map/all_gather | solution.py:51
  10.7 1.9 copy-start.4
  10.7 125.7 %copy-start.2 = (bf16[256,640]{1,0:T(8,128)(2,1)S(1)}, bf16[256,640]{1,0:T(8,128)(2,1)}, u32[]{:S(2)}) copy-start(bf16[256,640]{1,0:T(8,128)(2,1)} %param.9) | copy-start | bytes 983044
  11.8 124.5 %all-gather.6.cloned.1.call-start = ((), (), s32[]{:S(2)}) async-start(), calls=%async_computation.2 | async-start | bytes 6758400 | tf_op jit(solution)/shard_map/all_gather | solution.py:54
  12.6 248.0 %all-gather.8.cloned.1.call-start = ((), (), s32[]{:S(2)}) async-start(), calls=%async_computation.3 | async-start | bytes 10813440 | tf_op jit(solution)/shard_map/all_gather | solution.py:63
  142.3 14.1 %copy-start = (bf16[640,2,512]{2,1,0:T(2,128)(2,1)S(1)}, bf16[640,2,512]{2,1,0:T(2,128)(2,1)}, u32[]{:S(2)}) copy-start(bf16[640,2,512]{2,1,0:T(2,128)(2,1)} %param.17) | copy-start | bytes 3932164
  155.4 1.4 copy-start.5
  156.4 236.3 %reduce-scatter.2.cloned.1.call-start = ((), (), s32[]{:S(2)}) async-start(), calls=%async_computation.4 | async-start | bytes 18874368 | tf_op jit(solution)/shard_map/reduce_scatter | solution.py:76
  300.9 0.7 copy-start.6
  302.6 92.1 %copy-start.1 = (bf16[16,2,16,128]{3,2,1,0:T(8,128)(2,1)}, bf16[16,2,16,128]{3,2,1,0:T(8,128)(2,1)S(1)}, u32[]{:S(2)}) copy-start(bf16[16,2,16,128]{3,2,1,0:T(8,128)(2,1)S(1)} %scatter_fusion) | copy-start | bytes 393220
Sparse Core Ops, SparseCore 0:
  11.9 32.7 all-gather.3
  47.3 88.9 all-gather.5
  156.5 104.0 all-gather.7
  301.0 91.6 reduce-scatter.1
where the time goes:
time: 403 us
  waiting for transfers between devices  318 us (79%)
  matrix products  28.2 us (7%)
  other arithmetic  16 us (4%)
  between operations  13.9 us (3%)
  local copies, waits for them, and re-layouts  13.4 us (3%)
  blocking collectives  13.1 us (3%)
    all_gather x1, waiting for transfers between devices, shards(): every_row = lax.all_gather(normed, 'dp', axis=0, tiled=True)  104 us
    all_gather x1, waiting for transfers between devices, shards(): lax.all_gather(out_proj, 'dp', axis=0, tiled=True)  91.6 us
    reduce_scatter x1, waiting for transfers between devices, shards(): lax.psum_scatter(partial_sum.astype(jnp.float32).astype(jnp.bfloat16), 'm...  90.1 us
    all_gather x1, waiting for transfers between devices, shards(): all_heads = lax.all_gather(attended, 'mp', axis=1, tiled=True)  32.1 us
    dot_general x1, matrix products, shards(): jnp.dot(picked, flat_weights, preferred_element_type=jnp.float32)  19.9 us
    psum x1, blocking collectives, shards(): square_sums = lax.psum(jnp.sum(resid * resid, axis=1), 'mp')  13.1 us
    select_n x2, other arithmetic, shards(): jnp.take(packed_blocks, deal_order, axis=0)  10.2 us
    gather x1, local copies, waits for them, and re-layouts, shards(): jnp.take(packed_blocks, deal_order, axis=0)  10.2 us
  transfers between devices with their start and end apart: 4, of which 4 were waited for; matrix products, arithmetic and copies ran while one was open for 0% of the time, Pallas kernels for 0%

commit v1 on v0

--- a/solution.py
+++ b/solution.py
@@ -6,6 +6,19 @@
 D = 5120
 HD = 128
 epsilon = 1e-06
+
+
+def ring_gather(x, axis, dim):
+    ways = lax.axis_size(axis)
+    up = [(d, (d + 1) % ways) for d in range(ways)]
+    down = [(d, (d - 1) % ways) for d in range(ways)]
+    earlier, later = ([x], [x])
+    for _ in range(ways // 2):
+        earlier.append(lax.ppermute(earlier[-1], axis, up))
+    for _ in range((ways - 1) // 2):
+        later.append(lax.ppermute(later[-1], axis, down))
+    line = jnp.concatenate([*earlier[::-1], *later[1:]], axis=dim)
+    return jnp.roll(line, (lax.axis_index(axis) - ways // 2) * x.shape[dim], axis=dim)
 
 
 def attend(queries_in, key_values, request_ids):
@@ -48,7 +61,7 @@
     pages = key_values.reshape(2, pages_here, page_rows, channels).transpose(1, 0, 2, 3)
     kv_cache = jnp.zeros_like(pages).at[page_table % pages_here].set(pages)
     attended = attend(queries_in, key_values, request_ids)
-    all_heads = lax.all_gather(attended, "mp", axis=1, tiled=True)
+    all_heads = ring_gather(attended, "mp", 1)
     projected = jnp.dot(
         all_heads,
         lax.all_gather(out_proj, "dp", axis=0, tiled=True),

time: 403 us -> 370 us (0.918)
  waiting for transfers between devices: 318 us -> 255 us
  starting transfers between devices: 0.16 us -> 18.3 us
  local copies, waits for them, and re-layouts: 13.4 us -> 25.7 us
    all_gather x1, waiting for transfers between devices: 91.6 us -> 51.1 us  [shards(): lax.all_gather(out_proj, 'dp', axis=0, tiled=True)]
    all_gather x1 -> x0, waiting for transfers between devices: 32.1 us -> none  [shards(): all_heads = lax.all_gather(attended, 'mp', axis=1, tiled=True)]
    ppermute x0 -> x7, starting transfers between devices: none -> 18.2 us  [the longest x4 10.1 us: ring_gather(): earlier.append(lax.ppermute(earlier[-1], axis, up))]
    unnamed x16 -> x31, local copies, waits for them, and re-layouts: 2.13 us -> 13.7 us
    ppermute x0 -> x7, waiting for transfers between devices: none -> 9.28 us  [the longest x4 8.3 us: ring_gather(): earlier.append(lax.ppermute(earlier[-1], axis, up))]
  transfers between devices with their start and end apart: 4 -> 10, of which waited for: 4 -> 9; matrix products, arithmetic and copies ran while one was open for 0% -> 5% of each run, Pallas kernels for 0% -> 0%
where the time goes in v1:
time: 370 us
  waiting for transfers between devices  255 us (69%)
  matrix products  28.3 us (8%)
  local copies, waits for them, and re-layouts  25.7 us (7%)
  starting transfers between devices  18.3 us (5%)
  other arithmetic  15.9 us (4%)
  between operations  13.9 us (4%)
  blocking collectives  12.9 us (3%)
    all_gather x1, waiting for transfers between devices, shards(): every_row = lax.all_gather(normed, 'dp', axis=0, tiled=True)  104 us
    reduce_scatter x1, waiting for transfers between devices, shards(): lax.psum_scatter(partial_sum.astype(jnp.float32).astype(jnp.bfloat16), 'm...  89.8 us
    all_gather x1, waiting for transfers between devices, shards(): lax.all_gather(out_proj, 'dp', axis=0, tiled=True)  51.1 us
    dot_general x1, matrix products, shards(): jnp.dot(picked, flat_weights, preferred_element_type=jnp.float32)  19.9 us
    unnamed x31, local copies, waits for them, and re-layouts  13.7 us
    psum x1, blocking collectives, shards(): square_sums = lax.psum(jnp.sum(resid * resid, axis=1), 'mp')  12.9 us
    gather x1, local copies, waits for them, and re-layouts, shards(): jnp.take(packed_blocks, deal_order, axis=0)  10.2 us
    select_n x2, other arithmetic, shards(): jnp.take(packed_blocks, deal_order, axis=0)  10.1 us
  transfers between devices with their start and end apart: 10, of which 9 were waited for; matrix products, arithmetic and copies ran while one was open for 5% of the time, Pallas kernels for 0%

profile of v1, /device:TPU:1, one launch (start us, length us, event | category | flops | bytes accessed | tf_op | source)
XLA Modules:
  0.0 369.6 jit_solution(2981905237068109284)
XLA Ops:
  8.0 1.1 copy.16
  9.1 0.9 fusion.10
  10.0 1.2 fusion.18
  11.4 1.2 convolution_convert_fusion.1
  12.6 2.7 collective-permute-start
  15.3 4.0 %collective-permute-done = bf16[256,640]{0,1:T(8,128)(2,1)S(1)} collective-permute-done((bf16[256,640]{0,1:T(8,128)(2,1)S(1)}, bf16[256,640]{0,1:T(8,128)(2,1)S(1)}, u32[]{:S(2)}, u32[]{:S(2)}) %collective-permute-start) | collective-permute-done | bytes 327712 | tf_op jit(solution)/shard_map/ppermute | solution.py:17
  19.3 2.5 collective-permute-start.1
  21.8 1.7 collective-permute-start.4
  23.5 2.3 collective-permute-done.1
  25.8 2.5 collective-permute-start.2
  28.6 2.7 collective-permute-start.5
  31.2 1.1 collective-permute-done.2
  32.3 2.4 collective-permute-start.3
  35.5 3.7 %collective-permute-start.6 = (bf16[256,640]{0,1:T(8,128)(2,1)S(1)}, bf16[256,640]{0,1:T(8,128)(2,1)S(1)}, u32[]{:S(2)}, u32[]{:S(2)}) collective-permute-start(bf16[256,640]{0,1:T(8,128)(2,1)S(1)} %collective-permute-done.5), channel_id=1, source_target_pairs={{0,7},{1,0},{2,1},{3,2},{4,3},{5,4},{6,5},{7,6},{8,15},{9,8},{10,9... | collective-permute-start | bytes 983048 | tf_op jit(solution)/shard_map/ppermute | solution.py:19
  39.2 0.9 collective-permute-done.3
  40.8 0.8 constant_dynamic-update-slice_fusion.14
  43.8 0.8 constant_dynamic-update-slice_fusion.10
  45.3 0.8 constant_dynamic-update-slice_fusion.8
  49.1 0.8 constant_dynamic-update-slice_fusion.3
  52.1 51.1 %all-gather.3.cloned.1.call-done = bf16[5120,640]{1,0:T(8,128)(2,1)} async-done(((bf16[160,640]{1,0:T(8,128)(2,1)}), bf16[5120,640]{1,0:T(8,128)(2,1)}) %all-gather.3.cloned.1.call-update) | async-done | bytes 6553616 | tf_op jit(solution)/shard_map/all_gather | solution.py:67
  103.2 6.0 %multiply_reduce_fusion = (f32[256]{0:T(256)S(1)}, f32[256,640]{1,0:T(8,128)S(1)}) fusion(bf16[5120,640]{1,0:T(8,128)(2,1)} %all-gather.3.cloned.1.call-done, bf16[256,10240]{0,1:T(8,128)(2,1)} %constant_dynamic-update-slice_fusion, s32[]{:T(128)S(6)} %select_n.48, bf16[256,640]{1,0:T(8,128)(2,1)S(1)} %copy-done.2), kind=kOutput, calls=%fused_computation.18 | convolution fusion | flops 1678376704 | bytes 10159108 | tf_op jit(solution)/shard_map/dot_general | solution.py:65
  109.2 12.9 %psum.7 = f32[256]{0:T(256)S(1)} all-reduce(f32[256]{0:T(256)S(1)} %get-tuple-element.7), channel_id=1, replica_groups=mesh['dp'=32,'mp'=8] {'mp'}, use_global_device_ids=true, to_apply=%region_3.4 | all-reduce | flops 256 | bytes 2048 | tf_op jit(solution)/shard_map/psum | solution.py:71
  122.1 1.0 fusion.17
  123.5 103.8 %all-gather.5.cloned.1.call-done = bf16[8192,640]{1,0:T(8,128)(2,1)} async-done(((bf16[256,640]{1,0:T(8,128)(2,1)}), bf16[8192,640]{1,0:T(8,128)(2,1)}) %all-gather.5.cloned.1.call-update) | async-done | bytes 10485776 | tf_op jit(solution)/shard_map/all_gather | solution.py:76
  227.3 10.2 %gather_fusion = bf16[32,256,640]{2,1,0:T(8,128)(2,1)} fusion(bf16[32,256,640]{2,1,0:T(8,128)(2,1)} %bitcast.40, s32[1024]{0:T(1024)S(1)} %pad_clamp_fusion), kind=kCustom, calls=%fused_computation | custom fusion | bytes 20971648 | tf_op jit(solution)/shard_map/jit(_take)/gather | solution.py:82
  237.5 10.1 %broadcast_select_fusion = bf16[32,256,640]{2,1,0:T(8,128)(2,1)} fusion(bf16[32,256,640]{2,1,0:T(8,128)(2,1)} %gather_fusion, pred[32]{0:T(512)(128)(4,1)S(1)} %compare_and_fusion), kind=kLoop, calls=%fused_computation.3 | loop fusion | flops 5242880 | bytes 20971552 | tf_op jit(solution)/shard_map/jit(_take)/select_n | solution.py:82
  247.7 19.9 %convolution_convert_fusion = bf16[8192,1024]{1,0:T(8,128)(2,1)} fusion(bf16[8192,640]{1,0:T(8,128)(2,1)} %bitcast.41, bf16[640,1024]{1,0:T(8,128)(2,1)S(1)} %bitcast.44), kind=kOutput, calls=%fused_computation.2 | convolution fusion | flops 10745806848 | bytes 28573696 | tf_op jit(solution)/shard_map/dot_general | solution.py:85
  267.6 0.9 copy-done.3
  268.6 1.0 scatter_fusion
  269.6 89.8 %reduce-scatter.2.cloned.1.call-done = bf16[1024,1024]{1,0:T(8,128)(2,1)} async-done(((bf16[8192,1024]{1,0:T(8,128)(2,1)}), bf16[1024,1024]{1,0:T(8,128)(2,1)}) %reduce-scatter.2.cloned.1.call-update) | async-done | bytes 2097168 | tf_op jit(solution)/shard_map/reduce_scatter | solution.py:89
  359.4 2.0 convert_element_type.47
  361.4 1.7 fusion.2
  (44 shorter events, 11.4 us)
Async XLA Ops:
  7.2 27.6 %copy-start.4 = (bf16[640]{0:T(1024)(128)(2,1)S(1)}, bf16[640]{0:T(1024)(128)(2,1)}, u32[]{:S(2)}) copy-start(bf16[640]{0:T(1024)(128)(2,1)} %param.16) | copy-start | bytes 3844
  7.2 96.0 %all-gather.3.cloned.1.call-start = ((), (), s32[]{:S(2)}) async-start(), calls=%async_computation.1 | async-start | bytes 6758400 | tf_op jit(solution)/shard_map/all_gather | solution.py:67
  7.9 219.4 %all-gather.5.cloned.1.call-start = ((), (), s32[]{:S(2)}) async-start(), calls=%async_computation.2 | async-start | bytes 10813440 | tf_op jit(solution)/shard_map/all_gather | solution.py:76
  12.6 6.7 %collective-permute-start = (bf16[256,640]{0,1:T(8,128)(2,1)S(1)}, bf16[256,640]{0,1:T(8,128)(2,1)S(1)}, u32[]{:S(2)}, u32[]{:S(2)}) collective-permute-start(bf16[256,640]{0,1:T(8,128)(2,1)S(1)} %bitcast.45), channel_id=1, source_target_pairs={{0,1},{1,2},{2,3},{3,4},{4,5},{5,6},{6,7},{7,0},{8,9},{9,10},{10,1... | collective-permute-start | bytes 983048 | tf_op jit(solution)/shard_map/ppermute | solution.py:17
  19.3 6.5 %collective-permute-start.1 = (bf16[256,640]{0,1:T(8,128)(2,1)S(1)}, bf16[256,640]{0,1:T(8,128)(2,1)S(1)}, u32[]{:S(2)}, u32[]{:S(2)}) collective-permute-start(bf16[256,640]{0,1:T(8,128)(2,1)S(1)} %collective-permute-done), channel_id=1, source_target_pairs={{0,1},{1,2},{2,3},{3,4},{4,5},{5,6},{6,7},{7,0},{8,9},{9,10},{10,1... | collective-permute-start | bytes 983048 | tf_op jit(solution)/shard_map/ppermute | solution.py:17
  21.8 6.8 %collective-permute-start.4 = (bf16[256,640]{0,1:T(8,128)(2,1)S(1)}, bf16[256,640]{0,1:T(8,128)(2,1)S(1)}, u32[]{:S(2)}, u32[]{:S(2)}) collective-permute-start(bf16[256,640]{0,1:T(8,128)(2,1)S(1)} %bitcast.46), channel_id=1, source_target_pairs={{0,7},{1,0},{2,1},{3,2},{4,3},{5,4},{6,5},{7,6},{8,15},{9,8},{10,9... | collective-permute-start | bytes 983048 | tf_op jit(solution)/shard_map/ppermute | solution.py:19
  25.8 6.5 %collective-permute-start.2 = (bf16[256,640]{0,1:T(8,128)(2,1)S(1)}, bf16[256,640]{0,1:T(8,128)(2,1)S(1)}, u32[]{:S(2)}, u32[]{:S(2)}) collective-permute-start(bf16[256,640]{0,1:T(8,128)(2,1)S(1)} %collective-permute-done.1), channel_id=1, source_target_pairs={{0,1},{1,2},{2,3},{3,4},{4,5},{5,6},{6,7},{7,0},{8,9},{9,10},{10,1... | collective-permute-start | bytes 983048 | tf_op jit(solution)/shard_map/ppermute | solution.py:17
  28.6 6.9 %collective-permute-start.5 = (bf16[256,640]{0,1:T(8,128)(2,1)S(1)}, bf16[256,640]{0,1:T(8,128)(2,1)S(1)}, u32[]{:S(2)}, u32[]{:S(2)}) collective-permute-start(bf16[256,640]{0,1:T(8,128)(2,1)S(1)} %collective-permute-done.4), channel_id=1, source_target_pairs={{0,7},{1,0},{2,1},{3,2},{4,3},{5,4},{6,5},{7,6},{8,15},{9,8},{10,9... | collective-permute-start | bytes 983048 | tf_op jit(solution)/shard_map/ppermute | solution.py:19
  32.3 7.7 %collective-permute-start.3 = (bf16[256,640]{0,1:T(8,128)(2,1)S(1)}, bf16[256,640]{0,1:T(8,128)(2,1)S(1)}, u32[]{:S(2)}, u32[]{:S(2)}) collective-permute-start(bf16[256,640]{0,1:T(8,128)(2,1)S(1)} %collective-permute-done.2), channel_id=1, source_target_pairs={{0,1},{1,2},{2,3},{3,4},{4,5},{5,6},{6,7},{7,0},{8,9},{9,10},{10,1... | collective-permute-start | bytes 983048 | tf_op jit(solution)/shard_map/ppermute | solution.py:17
  34.8 68.4 %copy-start.2 = (bf16[256,640]{1,0:T(8,128)(2,1)S(1)}, bf16[256,640]{1,0:T(8,128)(2,1)}, u32[]{:S(2)}) copy-start(bf16[256,640]{1,0:T(8,128)(2,1)} %param.9) | copy-start | bytes 983044
  35.5 9.9 %collective-permute-start.6 = (bf16[256,640]{0,1:T(8,128)(2,1)S(1)}, bf16[256,640]{0,1:T(8,128)(2,1)S(1)}, u32[]{:S(2)}, u32[]{:S(2)}) collective-permute-start(bf16[256,640]{0,1:T(8,128)(2,1)S(1)} %collective-permute-done.5), channel_id=1, source_target_pairs={{0,7},{1,0},{2,1},{3,2},{4,3},{5,4},{6,5},{7,6},{8,15},{9,8},{10,9... | collective-permute-start | bytes 983048 | tf_op jit(solution)/shard_map/ppermute | solution.py:19
  52.1 71.0 %copy-start = (bf16[640,2,512]{2,1,0:T(2,128)(2,1)S(1)}, bf16[640,2,512]{2,1,0:T(2,128)(2,1)}, u32[]{:S(2)}) copy-start(bf16[640,2,512]{2,1,0:T(2,128)(2,1)} %param.17) | copy-start | bytes 3932164
  52.1 71.4 %copy-start.5 = (s32[32]{0:T(128)S(1)}, s32[32]{0:T(128)}, u32[]{:S(2)}) copy-start(s32[32]{0:T(128)} %param.13) | copy-start | bytes 388
  123.1 236.3 %reduce-scatter.2.cloned.1.call-start = ((), (), s32[]{:S(2)}) async-start(), calls=%async_computation.3 | async-start | bytes 18874368 | tf_op jit(solution)/shard_map/reduce_scatter | solution.py:89
  267.6 0.9 copy-start.3
  267.6 0.9 copy-start.6
  269.6 93.5 %copy-start.1 = (bf16[16,2,16,128]{3,2,1,0:T(8,128)(2,1)}, bf16[16,2,16,128]{3,2,1,0:T(8,128)(2,1)S(1)}, u32[]{:S(2)}) copy-start(bf16[16,2,16,128]{3,2,1,0:T(8,128)(2,1)S(1)} %scatter_fusion) | copy-start | bytes 393220
Sparse Core Ops, SparseCore 0:
  10.6 92.5 all-gather.2
  123.2 104.0 all-gather.4
  267.7 91.6 reduce-scatter.1
